TPU v7x, 256 devices: a whole 4x4x8 slice. The times are simulated.
256 devices in a mesh: space: 32 (over y, x, core), spin: 2 (over z_hi), cons: 4 (over z_lo).
Axes of the slice: x: 4, y: 4, z: 8 (z_hi: 2, z_lo: 4; z = z_hi * 4 + z_lo), core: 2. Of those that a mesh axis runs over, the one named last changes fastest.
Arguments:
- eigvecs: bfloat16 [2, 2, 256, 61440], P(None, None, None, 'space'), may hold values from -0.0234375 to 0.0234375
- solutions: bfloat16 [2, 2, 4, 256, 61440], P(None, None, 'spin', 'cons', 'space'), may hold values from -6 to 6
- elementals: bfloat16 [8, 2, 256, 256], replicated, may hold values from -0.375 to 0.375
- op_list: int32 [256, 16, 4], P(('space', 'spin', 'cons')), may hold values from 0 to 7, as said below
- live_count: int32 [256], P(('space', 'spin', 'cons')), may hold values from 1 to 16, as said below
Outputs:
- blocks: bfloat16 [2, 4096, 256, 256], P(None, ('space', 'spin', 'cons'))
Inputs may be any that keep to these rules, and one draw needn't show every extreme that they name: `op_list`: columns hold an elemental in 0 to 7, two sink spins in 0 to 3 and a sink slice in 0 to 1; slots at or beyond an owner's live count hold arbitrary entries of that kind. `live_count`: some owner has all 16 slots live.
All inputs are finite; a program needn't handle non-finite values.
Results may differ from a plain program's by a relative error of at most 0.0064.
Values may be sent and summed in bfloat16 or wider, within the bound.
A program may use at most 128 MiB of HBM per device.

v0:
```python
import jax
import jax.numpy as jnp
from jax import lax
from jax.sharding import PartitionSpec as P


def contract(left, phi, right):
    prod = jnp.einsum("pik,qkj->pqij", phi, right, preferred_element_type=jnp.float32)
    mixed = jnp.stack([prod[0, 0] - prod[1, 1], prod[0, 1] + prod[1, 0]]).astype(jnp.bfloat16)
    prod_two = jnp.einsum("pki,qkj->pqij", left, mixed, preferred_element_type=jnp.float32)
    scaled = jnp.stack(
        [prod_two[0, 0] + prod_two[1, 1], prod_two[0, 1] - prod_two[1, 0]]
    ) * left.shape[-1] ** (-0.5)
    return scaled.astype(jnp.bfloat16)


def body(eigvecs, solutions, elementals, op_list, live_count):
    prod = jnp.einsum("ptir,qtsjr->ptqsij", eigvecs, solutions, preferred_element_type=jnp.float32)
    partial_tau = jnp.stack([prod[0, :, 0] + prod[1, :, 1], prod[0, :, 1] - prod[1, :, 0]])
    summed_rows = lax.psum_scatter(partial_tau, "space", scatter_dimension=3, tiled=True).astype(
        jnp.bfloat16
    )
    tau_local = lax.all_gather(summed_rows, "space", axis=3, tiled=True)
    tau_spins = lax.all_gather(tau_local, "spin", axis=2, tiled=True)
    tau_full = lax.all_gather(tau_spins, "cons", axis=4, tiled=True)
    n_slices = tau_full.shape[1]
    n_vecs = tau_full.shape[3]
    flat = tau_full.reshape(2, n_slices * 4, n_vecs, n_vecs)
    items = op_list[0]
    count = live_count[0]
    n_slots = items.shape[0]

    def one_item(item):
        left = flat[:, item[3] * 4 + item[1]]
        right = flat[:, item[3] * 4 + item[2]]
        return contract(left, elementals[item[0]], right)

    results = jax.vmap(one_item, out_axes=1)(items)
    keep = jnp.arange(n_slots) < count
    blocks = jnp.where(keep[None, :, None, None], results, jnp.zeros_like(results))
    return blocks


def solution(mesh):
    return jax.shard_map(
        body,
        mesh=mesh,
        in_specs=(
            P(None, None, None, "space"),
            P(None, None, "spin", "cons", "space"),
            P(),
            P(("space", "spin", "cons"), None, None),
            P(("space", "spin", "cons")),
        ),
        out_specs=P(None, ("space", "spin", "cons"), None, None),
        check_vma=False,
    )
```

profile of v0, /device:TPU:1, one launch (start us, length us, event | category | flops | bytes accessed | tf_op | source)
XLA Modules:
  0.0 301.9 jit_solution(16725019120687271900)
XLA Ops:
  6.5 0.0 copy-start
  6.5 0.0 all-gather.2.cloned.1.call-start
  6.5 4.1 %fusion.17 = f32[2,2,2,2,256,64]{4,5,0,3,2,1:T(8,128)S(1)} fusion(bf16[2,2,256,1920]{3,2,1,0:T(8,128)(2,1)} %param.5, bf16[2,2,2,64,1920]{4,3,2,1,0:T(8,128)(2,1)} %param.6), kind=kOutput, calls=%fused_computation.30 | convolution fusion | flops 1006632960 | bytes 6946816 | tf_op jit(solution)/shard_map/ptir,qtsjr->ptqsij/dot_general | solution.py:18
  10.7 0.0 copy-start.3
  10.7 0.0 copy-start.2
  10.8 0.8 pad_maximum_fusion
  11.6 1.7 copy.36
  13.3 135.0 %all-reduce.2 = bf16[2,2,2,256,64]{4,2,1,0,3:T(2,128)(2,1)} all-reduce(f32[2,2,2,256,64]{4,2,1,0,3:T(2,128)S(1)} %copy.36), channel_id=2, replica_groups=mesh['space'=32,'spin'=2,'cons'=4] {'space'}, use_global_device_ids=true, to_apply=%region_0.0.clone | all-reduce | flops 131072 | bytes 786432
  148.3 0.0 copy-done.3
  148.3 0.6 dynamic-slice
  149.4 0.7 dynamic-slice_convert_fusion
  150.2 27.4 %all_gather.9 = bf16[2,2,2,256,64]{4,2,1,0,3:T(2,128)(2,1)S(1)} all-gather(bf16[2,2,2,8,64]{4,2,1,0,3:T(2,128)(2,1)S(1)} %dynamic-slice_convert_fusion), channel_id=1, replica_groups=mesh['space'=32,'spin'=2,'cons'=4] {'space'}, dimensions={3}, use_global_device_ids=true | all-gather | bytes 270336 | tf_op jit(solution)/shard_map/all_gather | solution.py:23
  177.6 0.5 copy.37
  178.1 15.3 %all_gather.10 = bf16[2,2,4,256,64]{3,4,1,0,2:T(8,128)(2,1)S(1)} all-gather(bf16[2,2,2,256,64]{3,4,1,0,2:T(8,128)(2,1)S(1)} %copy.37), channel_id=1, replica_groups=mesh['space'=32,'spin'=2,'cons'=4] {'spin'}, dimensions={2}, use_global_device_ids=true | all-gather | bytes 786432 | tf_op jit(solution)/shard_map/all_gather | solution.py:24
  193.4 1.2 copy.38
  194.6 0.0 all-gather.2.cloned.1.call-update
  195.2 0.0 copy-done.2
  195.3 0.0 copy-done
  195.3 2.8 gather_fusion.1
  198.0 50.3 %all-gather.2.cloned.1.call-done = bf16[2,2,4,256,256]{3,2,1,0,4:T(4,128)(2,1)} async-done(((bf16[2,2,4,256,64]{3,2,1,0,4:T(4,128)(2,1)}), bf16[2,2,4,256,256]{3,2,1,0,4:T(4,128)(2,1)}) %all-gather.2.cloned.1.call-update) | async-done | bytes 2097168 | tf_op jit(solution)/shard_map/all_gather | solution.py:25
  248.3 3.0 copy.39
  251.3 2.8 gather_fusion
  254.2 11.6 %convolution_bitcast_fusion.1 = f32[16,2,2,256,256]{3,4,1,2,0:T(8,128)} fusion(bf16[16,2,256,256]{3,2,1,0:T(8,128)(2,1)} %gather_fusion, bf16[16,2,256,256]{3,2,1,0:T(8,128)(2,1)} %gather_fusion.1), kind=kOutput, calls=%fused_computation.4 | convolution fusion | flops 2147483648 | bytes 25165824 | tf_op jit(solution)/shard_map/vmap(pik,qkj->pqij)/dot_general | solution.py:8
  265.8 5.5 %fusion.14 = bf16[1,16,256,256]{2,3,1,0:T(8,128)(2,1)} fusion(f32[16,2,2,256,256]{3,4,1,2,0:T(8,128)} %convolution_bitcast_fusion.1), kind=kLoop, calls=%fused_computation.27 | loop fusion | flops 2097152 | bytes 10485760 | tf_op jit(solution)/shard_map/vmap()/sub | solution.py:9
  271.3 5.4 %fusion.15 = bf16[1,16,256,256]{2,3,1,0:T(8,128)(2,1)} fusion(f32[16,2,2,256,256]{3,4,1,2,0:T(8,128)} %convolution_bitcast_fusion.1), kind=kLoop, calls=%fused_computation.28 | loop fusion | flops 2097152 | bytes 10485760 | tf_op jit(solution)/shard_map/vmap()/add | solution.py:9
  276.7 2.8 gather_fusion.2
  279.6 5.4 %convolution_bitcast_fusion = f32[16,2,2,256,256]{3,4,1,2,0:T(8,128)S(1)} fusion(bf16[16,2,256,256]{3,2,1,0:T(8,128)(2,1)} %gather_fusion.2, bf16[1,16,256,256]{2,3,1,0:T(8,128)(2,1)} %fusion.15, bf16[1,16,256,256]{2,3,1,0:T(8,128)(2,1)} %fusion.14), kind=kOutput, calls=%fused_computation.3 | convolution fusion | flops 2149580800 | bytes 25165824 | tf_op jit(solution)/shard_map/vmap(pki,qkj->pqij)/dot_general | solution.py:10
  285.0 0.5 fusion.2
  285.5 0.5 fusion.4
  286.1 0.0 copy-start.1
  286.1 2.8 fusion.1
  288.8 6.2 %copy.46 = bf16[2,16,256,256]{3,2,1,0:T(8,128)(2,1)} copy(bf16[2,16,256,256]{2,3,1,0:T(8,128)(2,1)} %fusion.1) | data formatting | bytes 8388608 | tf_op jit(solution)/shard_map/jit(_where)/select_n | solution.py:40
  295.0 0.0 copy-done.1
  (4 shorter events, 0.1 us)
Async XLA Ops:
  6.5 188.7 %copy-start = (bf16[8,2,256,256]{3,2,1,0:T(8,128)(2,1)S(1)}, bf16[8,2,256,256]{3,2,1,0:T(8,128)(2,1)}, u32[]{:S(2)}) copy-start(bf16[8,2,256,256]{3,2,1,0:T(8,128)(2,1)} %param.7) | copy-start | bytes 6291460
  6.5 241.8 %all-gather.2.cloned.1.call-start = ((), (), s32[]{:S(2)}) async-start(), calls=%async_computation | async-start | bytes 2621440 | tf_op jit(solution)/shard_map/all_gather | solution.py:25
  10.7 137.6 %copy-start.3 = (u32[256]{0:T(256)S(1)}, u32[256]{0:T(256)}, u32[]{:S(2)}) copy-start(u32[256]{0:T(256)} %constant.109) | copy-start | bytes 3076
  10.7 184.5 %copy-start.2 = (s32[1,16,4]{1,2,0:T(4,128)S(1)}, s32[1,16,4]{1,2,0:T(4,128)}, u32[]{:S(2)}) copy-start(s32[1,16,4]{1,2,0:T(4,128)} %param.8) | copy-start | bytes 772
  286.1 9.0 %copy-start.1 = (bf16[8,2,256,256]{3,2,1,0:T(8,128)(2,1)S(1)}, bf16[8,2,256,256]{3,2,1,0:T(8,128)(2,1)}, u32[]{:S(2)}) copy-start(bf16[8,2,256,256]{3,2,1,0:T(8,128)(2,1)} %param.7) | copy-start | bytes 6291460
Sparse Core Ops, SparseCore 0:
  194.7 53.5 all-gather.1
where the time goes:
time: 302 us
  blocking collectives  178 us (59%)
  waiting for transfers between devices  50.3 us (17%)
  local copies, waits for them, and re-layouts  22.3 us (7%)
  matrix products  21.2 us (7%)
  other arithmetic  15.7 us (5%)
  between operations  14.7 us (5%)
    unnamed x1, blocking collectives  135 us
    all_gather x1, waiting for transfers between devices, body(): tau_full = lax.all_gather(tau_spins, 'cons', axis=4, tiled=True)  50.3 us
    all_gather x1, blocking collectives, body(): tau_local = lax.all_gather(summed_rows, 'space', axis=3, tiled=True)  27.4 us
    all_gather x1, blocking collectives, body(): tau_spins = lax.all_gather(tau_local, 'spin', axis=2, tiled=True)  15.3 us
    dot_general x1, matrix products, contract(): jnp.einsum('pik,qkj->pqij', phi, right, preferred_element_type=jnp.float32)  11.6 us
    select_n x1, local copies, waits for them, and re-layouts, body(): jnp.where(keep[None, :, None, None], results, jnp.zeros_like(results))  6.19 us
  transfers between devices with their start and end apart: 1, of which 1 were waited for; matrix products, arithmetic and copies ran while one was open for 1% of the time, Pallas kernels for 0%

commit v1 on v0

v1 whole, which is shorter than its diff:
```python
import jax
import jax.numpy as jnp
from jax import lax
from jax.experimental import pallas as pl
from jax.experimental.pallas import tpu as pltpu
from jax.sharding import PartitionSpec as P

BF16 = jnp.bfloat16
F32 = jnp.float32
NT_DIMS = (((1,), (1,)), ((), ()))
SENDS = ((0, 0, 1), (0, 1, -1), (0, 1, 1), (0, 0, -1), (-1, 0, 1), (1, 1, -1))
LANDED = ((-1, 0), (1, 1), (-1, 1), (1, 0), (2, 0), (2, 1))


def wait_bytes(ref, sem):
    pltpu.make_async_copy(ref, ref, sem).wait()


def gather_kernel(eig, sol, tau, vbuf, sbuf, part, mine, recv, in_sem, rs_send, rs_recv, z_send, z_recv,
                  ring_send, ring_recv, chip_send, chip_recv):
    sp = lax.axis_index("space")
    z_hi = lax.axis_index("spin")
    z_lo = lax.axis_index("cons")
    core = lax.rem(sp, 2)
    chip = lax.div(sp, 2)
    x = lax.rem(chip, 4)
    y = lax.div(chip, 4)
    z = z_hi * 4 + z_lo
    re_im = lax.div(y, 2)
    half = lax.rem(y, 2)

    loads = []
    for t in range(2):
        loads.append((
            pltpu.make_async_copy(eig.at[:, t], vbuf.at[t], in_sem.at[2 * t]),
            pltpu.make_async_copy(sol.at[:, t], sbuf.at[t], in_sem.at[2 * t + 1]),
        ))
        for c in loads[t]:
            c.start()

    def at_space(d):
        return {"space": d}

    def at_z(d):
        return {"spin": lax.div(d, 4), "cons": lax.rem(d, 4)}

    barrier = pltpu.get_barrier_semaphore()

    def greet_plane(r, carry):
        pl.semaphore_signal(barrier, inc=1, device_id=at_space(lax.rem(sp + r, 32)))
        return carry

    def greet_z(r, carry):
        pl.semaphore_signal(barrier, inc=1, device_id=at_z(lax.rem(z + r, 8)))
        return carry

    lax.fori_loop(1, 32, greet_plane, 0)
    lax.fori_loop(1, 8, greet_z, 0)

    for t in range(2):
        for c in loads[t]:
            c.wait()
        v = vbuf[t].reshape(512, 1920)
        s = sbuf[t].reshape(256, 1920)
        prod = lax.dot_general(s, v, NT_DIMS, preferred_element_type=F32)
        re = prod[:128, :256] + prod[128:, 256:]
        im = prod[128:, :256] - prod[:128, 256:]
        re = re.reshape(8, 16, 256)
        im = im.reshape(8, 16, 256)
        mine[t, 0:8] = re
        mine[t, 8:16] = im
        part[t, 0:8] = re.astype(BF16)
        part[t, 8:16] = im.astype(BF16)
        if t == 0:
            pl.semaphore_wait(barrier, 38)

        def send(q, carry, t=t):
            p = lax.rem(chip + q, 16)
            d = 2 * p + t
            slot = lax.rem(sp - d + 32, 32) - 1

            @pl.when(d != sp)
            def _():
                pltpu.make_async_remote_copy(
                    src_ref=part.at[t, p], dst_ref=recv.at[slot], send_sem=rs_send, recv_sem=rs_recv,
                    device_id=at_space(d)).start()

            return carry

        lax.fori_loop(0, 16, send, 0)

    wait_bytes(recv, rs_recv)
    total = mine[core, chip]
    for k in range(31):
        total = total + recv[k].astype(F32)
    own = tau.at[core, re_im, z_hi, half, z_lo, x]
    own[...] = total.astype(BF16)

    def send_z(r, carry):
        pltpu.make_async_remote_copy(
            src_ref=own, dst_ref=own, send_sem=z_send, recv_sem=z_recv,
            device_id=at_z(lax.rem(z + r, 8))).start()
        return carry

    lax.fori_loop(1, 8, send_z, 0)

    def x_peer(k):
        return (y * 4 + lax.rem(x + k + 4, 4)) * 2 + core

    def y_peer(k):
        return (lax.rem(y + k + 4, 4) * 4 + x) * 2 + core

    def block_1x(k, h):
        return tau.at[core, re_im, 0, half, pl.ds(2 * h, 2), lax.rem(x + k + 4, 4)]

    def block_1y(k, h):
        yy = lax.rem(y + k + 4, 4)
        return tau.at[core, lax.div(yy, 2), 1, lax.rem(yy, 2), pl.ds(2 * h, 2), x]

    def block_2y(k, h):
        yy = lax.rem(y + k + 4, 4)
        return tau.at[core, lax.div(yy, 2), 0, lax.rem(yy, 2), pl.ds(2 * h, 2)]

    def block_2x(k, h):
        return tau.at[core, :, 1, :, pl.ds(2 * h, 2), lax.rem(x + k + 4, 4)]

    class Ring:
        def __init__(self, i, block, peer):
            self.i, self.block, self.peer = i, block, peer

        def copy(self, n, ref, step):
            return pltpu.make_async_remote_copy(
                src_ref=ref, dst_ref=ref, send_sem=ring_send.at[self.i, n], recv_sem=ring_recv.at[self.i, n],
                device_id=at_space(self.peer(step)))

        def send(self, n):
            k, h, step = SENDS[n]
            return self.copy(n, self.block(k, h), step)

        def landed(self, n):
            return self.block(*LANDED[n])

        def start(self):
            for n in range(4):
                self.send(n).start()

        def wait(self, n):
            wait_bytes(self.landed(n), ring_recv.at[self.i, n])

        def forward(self):
            self.wait(0)
            self.send(4).start()
            self.wait(1)
            self.send(5).start()

        def drain(self):
            for n in range(6):
                self.send(n).wait_send()

    ring_1x = Ring(0, block_1x, x_peer)
    ring_1y = Ring(1, block_1y, y_peer)
    ring_2y = Ring(2, block_2y, y_peer)
    ring_2x = Ring(3, block_2x, x_peer)

    partner = sp + 1 - 2 * core

    def chip_copy(n, ref):
        return pltpu.make_async_remote_copy(
            src_ref=ref, dst_ref=ref, send_sem=chip_send.at[n], recv_sem=chip_recv.at[n],
            device_id=at_space(partner))

    wait_bytes(recv.at[pl.ds(0, 7)], z_recv)
    ring_1x.start()
    ring_1y.start()
    ring_1x.forward()
    ring_1y.forward()
    for n in range(2, 6):
        ring_1x.wait(n)
    ring_2y.start()
    for n in range(2, 6):
        ring_1y.wait(n)
    ring_2x.start()
    shares = [block_2y(0, 0), block_2y(0, 1), block_2x(0, 0), block_2x(0, 1)]
    for n in range(4):
        chip_copy(n, shares[n]).start()
    ring_2y.forward()
    ring_2x.forward()
    for n in range(6):
        for ring in (ring_2y, ring_2x):
            if n >= 2:
                ring.wait(n)
            shares.append(ring.landed(n))
            chip_copy(len(shares) - 1, shares[-1]).start()
    for n in range(len(shares)):
        wait_bytes(shares[n], chip_recv.at[n])
    wait_bytes(recv, rs_send)
    wait_bytes(recv.at[pl.ds(0, 7)], z_send)
    for ring in (ring_1x, ring_1y, ring_2y, ring_2x):
        ring.drain()
    for n in range(len(shares)):
        chip_copy(n, shares[n]).wait_send()


def gather_tau(eigvecs, solutions):
    return pl.pallas_call(
        gather_kernel,
        out_shape=pltpu.VMEM((2, 2, 2, 2, 4, 4, 16, 256), BF16),
        in_specs=[pl.BlockSpec(memory_space=pltpu.HBM)] * 2,
        out_specs=pl.BlockSpec(memory_space=pltpu.VMEM),
        scratch_shapes=[
            pltpu.VMEM((2, 2, 256, 1920), BF16),
            pltpu.VMEM((2, 2, 2, 64, 1920), BF16),
            pltpu.VMEM((2, 16, 16, 256), BF16),
            pltpu.VMEM((2, 16, 16, 256), F32),
            pltpu.VMEM((31, 16, 256), BF16),
            pltpu.SemaphoreType.DMA((4,)),
            pltpu.SemaphoreType.DMA,
            pltpu.SemaphoreType.DMA,
            pltpu.SemaphoreType.DMA,
            pltpu.SemaphoreType.DMA,
            pltpu.SemaphoreType.DMA((4, 6)),
            pltpu.SemaphoreType.DMA((4, 6)),
            pltpu.SemaphoreType.DMA((16,)),
            pltpu.SemaphoreType.DMA((16,)),
        ],
        compiler_params=pltpu.CompilerParams(collective_id=0, has_side_effects=True, vmem_limit_bytes=24 << 20),
        name="gather_tau",
    )(eigvecs, solutions)


def blocks_kernel(items, count, tau, elem, out, buf, sem):
    n_slots = 16

    def put(k):
        return pltpu.make_async_copy(buf.at[lax.rem(k, 4)], out.at[:, k], sem.at[lax.rem(k, 4)])

    def one(k, carry):
        e = items[k, 0]
        a = items[k, 1]
        b = items[k, 2]
        t = items[k, 3]
        slot = lax.rem(k, 4)

        @pl.when(k >= 4)
        def _():
            put(k - 4).wait()

        @pl.when(k < count[0])
        def _():
            phi_re, phi_im = elem[e, 0], elem[e, 1]
            phi = jnp.concatenate([
                jnp.concatenate([phi_re, -phi_im], axis=1),
                jnp.concatenate([phi_im, phi_re], axis=1)], axis=0)
            right = jnp.concatenate([tau[t, 0, b], tau[t, 1, b]], axis=1)
            mixed = lax.dot_general(phi, right, NT_DIMS, preferred_element_type=F32).astype(BF16)
            left_re, left_im = tau[t, 0, a], tau[t, 1, a]
            left = jnp.concatenate([
                jnp.concatenate([left_re, left_im], axis=1),
                jnp.concatenate([-left_im, left_re], axis=1)], axis=0)
            res = jnp.dot(left, mixed, preferred_element_type=F32) * (256.0 ** -0.5)
            buf[slot] = res.astype(BF16).reshape(2, 256, 256)

        @pl.when(k >= count[0])
        def _():
            buf[slot] = jnp.zeros((2, 256, 256), BF16)

        put(k).start()
        return carry

    lax.fori_loop(0, n_slots, one, 0)
    for k in range(n_slots - 4, n_slots):
        put(k).wait()


def make_blocks(items, count, tau, elementals):
    return pl.pallas_call(
        blocks_kernel,
        out_shape=jax.ShapeDtypeStruct((2, 16, 256, 256), BF16),
        in_specs=[
            pl.BlockSpec(memory_space=pltpu.SMEM),
            pl.BlockSpec(memory_space=pltpu.SMEM),
            pl.BlockSpec(memory_space=pltpu.VMEM),
            pl.BlockSpec(memory_space=pltpu.VMEM),
        ],
        out_specs=pl.BlockSpec(memory_space=pl.ANY),
        scratch_shapes=[pltpu.VMEM((4, 2, 256, 256), BF16), pltpu.SemaphoreType.DMA((4,))],
        compiler_params=pltpu.CompilerParams(vmem_limit_bytes=24 << 20),
        name="make_blocks",
    )(items, count, tau, elementals)


def body(eigvecs, solutions, elementals, op_list, live_count):
    tau = gather_tau(eigvecs, solutions).reshape(2, 2, 4, 256, 256)
    return make_blocks(op_list[0], live_count, tau, elementals)


def solution(mesh):
    return jax.shard_map(
        body,
        mesh=mesh,
        in_specs=(
            P(None, None, None, "space"),
            P(None, None, "spin", "cons", "space"),
            P(),
            P(("space", "spin", "cons"), None, None),
            P(("space", "spin", "cons")),
        ),
        out_specs=P(None, ("space", "spin", "cons"), None, None),
        check_vma=False,
    )
```

time: 302 us -> 56.4 us (0.19)
  blocking collectives: 178 us -> 0 us
  Pallas kernels: 0 us -> 51.6 us
  waiting for transfers between devices: 50.3 us -> 0 us
  matrix products: 21.2 us -> 0 us
  local copies, waits for them, and re-layouts: 22.3 us -> 4.42 us
  other arithmetic: 15.7 us -> 0 us
  between operations: 14.7 us -> 0.67 us
    unnamed x1 -> x0, blocking collectives: 135 us -> none
    pallas_call x0 -> x2, Pallas kernels: none -> 51.6 us  [the longest x1 39.6 us: gather_tau(): pl.pallas_call(gather_kernel, out_shape=pltpu.VMEM((2, 2, 2, 2, 4, 4, 16,...]
    all_gather x1 -> x0, waiting for transfers between devices: 50.3 us -> none  [body(): tau_full = lax.all_gather(tau_spins, 'cons', axis=4, tiled=True)]
    all_gather x2 -> x0, blocking collectives: 42.7 us -> none  [the longest x1 27.4 us: body(): tau_local = lax.all_gather(summed_rows, 'space', axis=3, tiled=True)]
    dot_general x3 -> x0, matrix products: 21.2 us -> none  [the longest x1 11.6 us: contract(): jnp.einsum('pik,qkj->pqij', phi, right, preferred_element_type=jnp.float32)]
    gather x3 -> x0, local copies, waits for them, and re-layouts: 8.41 us -> none  [the longest x1 2.83 us: one_item(): right = flat[:, item[3] * 4 + item[2]]]
    select_n x1 -> x0, local copies, waits for them, and re-layouts: 6.19 us -> none  [body(): jnp.where(keep[None, :, None, None], results, jnp.zeros_like(results))]
    sub x3 -> x0, other arithmetic: 6.11 us -> none  [the longest x1 5.53 us: contract(): prod[0, 0] - prod[1, 1]]
  transfers between devices with their start and end apart: 1 -> 0, of which waited for: 1 -> 0; matrix products, arithmetic and copies ran while one was open for 1% -> 0% of each run, Pallas kernels for 0% -> 0%
where the time goes in v1:
time: 56.4 us; the launch traced here: 56.7 us
  Pallas kernels  51.6 us (91%)
  local copies, waits for them, and re-layouts  4.42 us (8%)
  between operations  0.67 us (1%)
    pallas_call x1, Pallas kernels, gather_tau(): pl.pallas_call(gather_kernel, out_shape=pltpu.VMEM((2, 2, 2, 2, 4, 4, 16,...  39.6 us
    pallas_call x1, Pallas kernels, make_blocks(): pl.pallas_call(blocks_kernel, out_shape=jax.ShapeDtypeStruct((2, 16, 256,...  12 us
    unnamed x6, local copies, waits for them, and re-layouts  3.66 us

profile of v1, /device:TPU:1, one launch (start us, length us, event | category | flops | bytes accessed | tf_op | source)
XLA Modules:
  0.0 56.7 jit_solution(16476327253560068071)
XLA Ops:
  0.7 0.8 %copy.6.items = s32[16,4]{1,0:T(8,128)S(1)} copy(s32[16,4]{0,1:T(4,128)} %bitcast.3) | data formatting | bytes 512 | tf_op jit(solution)/shard_map/squeeze | solution.py:294
  1.4 0.0 copy-start
  1.4 2.1 %copy-done = bf16[2,2,256,1920]{3,2,1,0:T(8,128)(2,1)S(1)} copy-done((bf16[2,2,256,1920]{3,2,1,0:T(8,128)(2,1)S(1)}, bf16[2,2,256,1920]{3,2,1,0:T(8,128)(2,1)}, u32[]{:S(2)}) %copy-start) | copy-done | bytes 3932184
  3.5 0.0 copy-start.2
  3.5 1.5 %copy-done.2 = bf16[2,2,2,64,1920]{4,3,2,1,0:T(8,128)(2,1)S(1)} copy-done((bf16[2,2,2,64,1920]{4,3,2,1,0:T(8,128)(2,1)S(1)}, bf16[2,2,2,64,1920]{4,3,2,1,0:T(8,128)(2,1)}, u32[]{:S(2)}) %copy-start.2) | copy-done | bytes 1966104
  5.1 0.0 copy-start.1
  5.1 39.6 %gather_tau.1 = bf16[2,2,2,2,4,4,16,256]{7,6,5,4,3,2,1,0:T(8,128)(2,1)S(1)} custom-call(bf16[2,2,256,1920]{3,2,1,0:T(8,128)(2,1)S(1)} %copy-done, bf16[2,2,2,64,1920]{4,3,2,1,0:T(8,128)(2,1)S(1)} %copy-done.2), custom_call_target="tpu_custom_call" | custom-call | tf_op jit(solution)/shard_map/gather_tau/pallas_call | solution.py:205
  44.6 0.0 copy-done.1
  44.7 12.0 %make_blocks.1 = bf16[2,16,256,256]{3,2,1,0:T(8,128)(2,1)} custom-call(s32[16,4]{1,0:T(8,128)S(1)} %copy.6.items, s32[1]{0:T(128)S(6)} %copy.7.count, bf16[2,2,4,256,256]{4,3,2,1,0:T(8,128)(2,1)S(1)} %bitcast.2, bf16[8,2,256,256]{3,2,1,0:T(8,128)(2,1)S(1)} %copy-done.1), custom_call_target="tpu_custom_call" | custom-call | tf_op jit(solution)/shard_map/make_blocks/pallas_call | solution.py:276
Async XLA Ops:
  1.4 2.1 %copy-start = (bf16[2,2,256,1920]{3,2,1,0:T(8,128)(2,1)S(1)}, bf16[2,2,256,1920]{3,2,1,0:T(8,128)(2,1)}, u32[]{:S(2)}) copy-start(bf16[2,2,256,1920]{3,2,1,0:T(8,128)(2,1)} %eig.1) | copy-start | bytes 11796484
  3.5 1.5 %copy-start.2 = (bf16[2,2,2,64,1920]{4,3,2,1,0:T(8,128)(2,1)S(1)}, bf16[2,2,2,64,1920]{4,3,2,1,0:T(8,128)(2,1)}, u32[]{:S(2)}) copy-start(bf16[2,2,2,64,1920]{4,3,2,1,0:T(8,128)(2,1)} %sol.1) | copy-start | bytes 5898244
  5.1 39.6 %copy-start.1 = (bf16[8,2,256,256]{3,2,1,0:T(8,128)(2,1)S(1)}, bf16[8,2,256,256]{3,2,1,0:T(8,128)(2,1)}, u32[]{:S(2)}) copy-start(bf16[8,2,256,256]{3,2,1,0:T(8,128)(2,1)} %elem.1) | copy-start | bytes 6291460

commit v2 on v0

v2 whole, which is shorter than its diff:
```python
import jax
import jax.numpy as jnp
from jax import lax
from jax.experimental import pallas as pl
from jax.experimental.pallas import tpu as pltpu
from jax.sharding import PartitionSpec as P

BF16 = jnp.bfloat16
F32 = jnp.float32
NT_DIMS = (((1,), (1,)), ((), ()))
OTHERS = sorted(
    [(dx, dy) for dx in range(4) for dy in range(4) if dx or dy],
    key=lambda d: -(min(d[0], 4 - d[0]) + min(d[1], 4 - d[1])))
PLANES = (4, 3, 5, 2, 6, 1, 7)
LINES = (0, 1, 3, 2)


def wait_bytes(ref, sem):
    pltpu.make_async_copy(ref, ref, sem).wait()


def gather_kernel(eig, sol, tau, vbuf, sbuf, give, take, mine, part, recv, in_sem, pair_send, pair_recv,
                  sum_send, sum_recv, z_send, z_recv, one_send, one_recv, two_send, pass_send, two_recv,
                  chip_send, chip_recv):
    sp = lax.axis_index("space")
    z_hi = lax.axis_index("spin")
    z_lo = lax.axis_index("cons")
    core = lax.rem(sp, 2)
    chip = lax.div(sp, 2)
    x = lax.rem(chip, 4)
    y = lax.div(chip, 4)
    z = z_hi * 4 + z_lo

    def load(n):
        t = 1 - core if n == 0 else core
        return [
            pltpu.make_async_copy(src.at[p, t], dst.at[n, p], in_sem.at[n, p, i])
            for p in range(2) for i, (src, dst) in enumerate(((eig, vbuf), (sol, sbuf)))]

    loads = [load(0), load(1)]
    for c in loads[0] + loads[1]:
        c.start()

    def at_chip(dx, dy):
        return {"space": (lax.rem(y + dy, 4) * 4 + lax.rem(x + dx, 4)) * 2 + core}

    def at_plane(r):
        d = lax.rem(z + r, 8)
        return {"spin": lax.div(d, 4), "cons": lax.rem(d, 4)}

    partner = {"space": sp + 1 - 2 * core}
    everyone = [partner] + [at_chip(*d) for d in OTHERS] + [at_plane(r) for r in PLANES]
    barrier = pltpu.get_barrier_semaphore()
    for d in everyone:
        pl.semaphore_signal(barrier, inc=1, device_id=d)

    def remote(src, dst, send, recv, device):
        return pltpu.make_async_remote_copy(src_ref=src, dst_ref=dst, send_sem=send, recv_sem=recv, device_id=device)

    def partial(n):
        for c in loads[n]:
            c.wait()
        v = vbuf[n].reshape(512, 1920)
        s = sbuf[n].reshape(256, 1920)
        prod = lax.dot_general(s, v, NT_DIMS, preferred_element_type=F32)
        re = prod[:128, :256] + prod[128:, 256:]
        im = prod[128:, :256] - prod[:128, 256:]
        return re.reshape(8, 16, 256), im.reshape(8, 16, 256)

    give[0:8], give[8:16] = partial(0)
    pl.semaphore_wait(barrier, len(everyone))
    remote(give, take, pair_send, pair_recv, partner).start()
    mine[0:8], mine[8:16] = partial(1)
    wait_bytes(take, pair_recv)
    both = mine[...] + take[...]
    mine[...] = both
    part[...] = both.astype(BF16)
    for n, (dx, dy) in enumerate(OTHERS):
        remote(part.at[lax.rem(y + dy, 4) * 4 + lax.rem(x + dx, 4)], recv.at[n], sum_send, sum_recv,
               at_chip(dx, dy)).start()
    wait_bytes(recv, sum_recv)
    total = mine[chip]
    for n in range(15):
        total = total + recv[n].astype(F32)

    def piece(r, dx=0, dy=0):
        zz = lax.rem(z + r, 8)
        yy = lax.rem(y + dy, 4)
        return tau.at[core, lax.div(yy, 2), lax.div(zz, 4), lax.rem(yy, 2), lax.rem(zz, 4), lax.rem(x + dx, 4)]

    own = piece(0)
    own[...] = total.astype(BF16)
    for r in PLANES:
        remote(own, own, z_send, z_recv.at[r - 1], at_plane(r)).start()

    def spread(r):
        hi = lax.div(lax.rem(z + r, 8), 4)
        for k in (2, 1, 3):
            xx = lax.rem(x + k * (1 - hi), 4)
            yy = lax.rem(y + k * hi, 4)
            remote(piece(r), piece(r), one_send, one_recv.at[hi, k - 1],
                   {"space": (yy * 4 + xx) * 2 + core}).start()

    spread(0)
    for r in reversed(PLANES):
        wait_bytes(piece(r), z_recv.at[8 - r - 1])
        spread(r)

    def line(hi, k, step):
        dx, dy = (k, step) if hi == 0 else (step, k)
        yy = lax.rem(y + dy, 4)
        return tau.at[core, lax.div(yy, 2), hi, lax.rem(yy, 2), :, lax.rem(x + dx, 4)]

    def ring_peer(hi, step):
        return at_chip(0, step) if hi == 0 else at_chip(step, 0)

    def two(hi, k, n, step, send, to):
        ref = line(hi, k, step)
        return remote(ref, ref, send, two_recv.at[hi, k, n], ring_peer(hi, to))

    def share(ref):
        remote(ref, ref, chip_send, chip_recv, partner).start()

    def begin(hi, k):
        if k:
            wait_bytes(line(hi, k, 0), one_recv.at[hi, 4 - k - 1])
        two(hi, k, 0, 0, two_send, 1).start()
        two(hi, k, 1, 0, two_send, 3).start()
        share(line(hi, k, 0))

    def landed(hi, k, n):
        step = (3, 1, 2)[n]
        wait_bytes(line(hi, k, step), two_recv.at[hi, k, n])
        if n == 0 and k in (0, 2):
            two(hi, k, 2, 3, pass_send, 1).start()
        if n == 1 and k in (1, 3):
            two(hi, k, 2, 1, pass_send, 3).start()
        share(line(hi, k, step))

    for k in LINES:
        for hi in range(2):
            begin(hi, k)
    for k in LINES:
        for n in range(2):
            for hi in range(2):
                landed(hi, k, n)
    for k in LINES:
        for hi in range(2):
            landed(hi, k, 2)
    wait_bytes(tau.at[1 - core], chip_recv)
    wait_bytes(give, pair_send)
    wait_bytes(recv, sum_send)
    wait_bytes(recv.at[pl.ds(0, 7)], z_send)
    wait_bytes(give.at[pl.ds(0, 12)], one_send)
    wait_bytes(tau.at[core, 0], two_send)
    wait_bytes(tau.at[core, 0, 0], pass_send)
    wait_bytes(tau.at[core], chip_send)


def gather_tau(eigvecs, solutions):
    dma = pltpu.SemaphoreType.DMA
    return pl.pallas_call(
        gather_kernel,
        out_shape=pltpu.VMEM((2, 2, 2, 2, 4, 4, 16, 256), BF16),
        in_specs=[pl.BlockSpec(memory_space=pltpu.HBM)] * 2,
        out_specs=pl.BlockSpec(memory_space=pltpu.VMEM),
        scratch_shapes=[
            pltpu.VMEM((2, 2, 256, 1920), BF16),
            pltpu.VMEM((2, 2, 2, 64, 1920), BF16),
            pltpu.VMEM((16, 16, 256), F32),
            pltpu.VMEM((16, 16, 256), F32),
            pltpu.VMEM((16, 16, 256), F32),
            pltpu.VMEM((16, 16, 256), BF16),
            pltpu.VMEM((15, 16, 256), BF16),
            dma((2, 2, 2)),
            dma, dma,
            dma, dma,
            dma, dma((7,)),
            dma, dma((2, 3)),
            dma, dma, dma((2, 4, 3)),
            dma, dma,
        ],
        compiler_params=pltpu.CompilerParams(collective_id=0, has_side_effects=True, vmem_limit_bytes=24 << 20),
        name="gather_tau",
    )(pltpu.with_memory_space_constraint(eigvecs, pltpu.HBM), pltpu.with_memory_space_constraint(solutions, pltpu.HBM))


def blocks_kernel(items, count, tau, elem, out, buf, sem):
    n_slots = 16

    def put(k):
        return pltpu.make_async_copy(buf.at[lax.rem(k, 4)], out.at[:, k], sem.at[lax.rem(k, 4)])

    def mix(k):
        e = items[0, k]
        b = items[2, k]
        t = items[3, k]
        phi_re, phi_im = elem[e, 0], elem[e, 1]
        phi = jnp.concatenate([
            jnp.concatenate([phi_re, -phi_im], axis=1),
            jnp.concatenate([phi_im, phi_re], axis=1)], axis=0)
        right = jnp.concatenate([tau[t, 0, b], tau[t, 1, b]], axis=1)
        return lax.dot_general(phi, right, NT_DIMS, preferred_element_type=F32).astype(BF16)

    def finish(k, mixed):
        a = items[1, k]
        t = items[3, k]
        left_re, left_im = tau[t, 0, a], tau[t, 1, a]
        left = jnp.concatenate([
            jnp.concatenate([left_re, left_im], axis=1),
            jnp.concatenate([-left_im, left_re], axis=1)], axis=0)
        res = jnp.dot(left, mixed, preferred_element_type=F32) * (256.0 ** -0.5)
        return jnp.where(k < count[0], res, 0.0).astype(BF16).reshape(2, 256, 256)

    def two(n, carry):
        k = 2 * n

        @pl.when(n >= 2)
        def _():
            put(k - 4).wait()
            put(k - 3).wait()

        @pl.when(k < count[0])
        def _():
            mixed = [mix(k), mix(k + 1)]
            for i in range(2):
                buf[lax.rem(k + i, 4)] = finish(k + i, mixed[i])

        @pl.when(k >= count[0])
        def _():
            for i in range(2):
                buf[lax.rem(k + i, 4)] = jnp.zeros((2, 256, 256), BF16)

        put(k).start()
        put(k + 1).start()
        return carry

    lax.fori_loop(0, n_slots // 2, two, 0)
    for k in range(n_slots - 4, n_slots):
        put(k).wait()


def make_blocks(items, count, tau, elementals):
    return pl.pallas_call(
        blocks_kernel,
        out_shape=jax.ShapeDtypeStruct((2, 16, 256, 256), BF16),
        in_specs=[
            pl.BlockSpec(memory_space=pltpu.SMEM),
            pl.BlockSpec(memory_space=pltpu.SMEM),
            pl.BlockSpec(memory_space=pltpu.VMEM),
            pl.BlockSpec(memory_space=pltpu.VMEM),
        ],
        out_specs=pl.BlockSpec(memory_space=pl.ANY),
        scratch_shapes=[pltpu.VMEM((4, 2, 256, 256), BF16), pltpu.SemaphoreType.DMA((4,))],
        compiler_params=pltpu.CompilerParams(vmem_limit_bytes=24 << 20),
        name="make_blocks",
    )(items, count, tau, elementals)


def body(eigvecs, solutions, elementals, op_list, live_count):
    tau = gather_tau(eigvecs, solutions).reshape(2, 2, 4, 256, 256)
    return make_blocks(op_list[0].T, live_count, tau, elementals)


def solution(mesh):
    return jax.shard_map(
        body,
        mesh=mesh,
        in_specs=(
            P(None, None, None, "space"),
            P(None, None, "spin", "cons", "space"),
            P(),
            P(("space", "spin", "cons"), None, None),
            P(("space", "spin", "cons")),
        ),
        out_specs=P(None, ("space", "spin", "cons"), None, None),
        check_vma=False,
    )
```

time: 302 us -> 42.1 us (0.14)
  blocking collectives: 178 us -> 0 us
  waiting for transfers between devices: 50.3 us -> 0 us
  Pallas kernels: 0 us -> 40.9 us
  local copies, waits for them, and re-layouts: 22.3 us -> 0.01 us
  matrix products: 21.2 us -> 0 us
  other arithmetic: 15.7 us -> 0 us
  between operations: 14.7 us -> 0.69 us
    unnamed x1 -> x0, blocking collectives: 135 us -> none
    all_gather x1 -> x0, waiting for transfers between devices: 50.3 us -> none  [body(): tau_full = lax.all_gather(tau_spins, 'cons', axis=4, tiled=True)]
    all_gather x2 -> x0, blocking collectives: 42.7 us -> none  [the longest x1 27.4 us: body(): tau_local = lax.all_gather(summed_rows, 'space', axis=3, tiled=True)]
    pallas_call x0 -> x2, Pallas kernels: none -> 40.9 us  [the longest x1 34.3 us: gather_tau(): pl.pallas_call(gather_kernel, out_shape=pltpu.VMEM((2, 2, 2, 2, 4, 4, 16,...]
    dot_general x3 -> x0, matrix products: 21.2 us -> none  [the longest x1 11.6 us: contract(): jnp.einsum('pik,qkj->pqij', phi, right, preferred_element_type=jnp.float32)]
    gather x3 -> x0, local copies, waits for them, and re-layouts: 8.41 us -> none  [the longest x1 2.83 us: one_item(): right = flat[:, item[3] * 4 + item[2]]]
    select_n x1 -> x0, local copies, waits for them, and re-layouts: 6.19 us -> none  [body(): jnp.where(keep[None, :, None, None], results, jnp.zeros_like(results))]
    sub x3 -> x0, other arithmetic: 6.11 us -> none  [the longest x1 5.53 us: contract(): prod[0, 0] - prod[1, 1]]
  transfers between devices with their start and end apart: 1 -> 0, of which waited for: 1 -> 0; matrix products, arithmetic and copies ran while one was open for 1% -> 0% of each run, Pallas kernels for 0% -> 0%
where the time goes in v2:
time: 42.1 us; the launch traced here: 41.6 us
  Pallas kernels  40.9 us (97%)
  between operations  0.69 us (2%)
    pallas_call x1, Pallas kernels, gather_tau(): pl.pallas_call(gather_kernel, out_shape=pltpu.VMEM((2, 2, 2, 2, 4, 4, 16,...  34.3 us
    pallas_call x1, Pallas kernels, make_blocks(): pl.pallas_call(blocks_kernel, out_shape=jax.ShapeDtypeStruct((2, 16, 256,...  6.67 us

profile of v2, /device:TPU:1, one launch (start us, length us, event | category | flops | bytes accessed | tf_op | source)
XLA Modules:
  0.0 41.6 jit_solution(5082183315813137096)
XLA Ops:
  0.7 0.0 copy-start
  0.7 0.0 copy-start.1
  0.7 34.3 %gather_tau.1 = bf16[2,2,2,2,4,4,16,256]{7,6,5,4,3,2,1,0:T(8,128)(2,1)S(1)} custom-call(bf16[2,2,256,1920]{3,2,1,0:T(8,128)(2,1)} %eig.1, bf16[2,2,2,64,1920]{4,3,2,1,0:T(8,128)(2,1)} %sol.1), custom_call_target="tpu_custom_call" | custom-call | tf_op jit(solution)/shard_map/gather_tau/pallas_call | solution.py:162
  34.9 0.0 copy-done
  34.9 0.0 copy-done.1
  35.0 6.7 %make_blocks.1 = bf16[2,16,256,256]{3,2,1,0:T(8,128)(2,1)} custom-call(s32[4,16]{1,0:T(4,128)S(1)} %bitcast.5, s32[1]{0:T(128)S(6)} %copy.6.count, bf16[2,2,4,256,256]{4,3,2,1,0:T(8,128)(2,1)S(1)} %bitcast.4, bf16[8,2,256,256]{3,2,1,0:T(8,128)(2,1)S(1)} %copy-done), custom_call_target="tpu_custom_call" | custom-call | tf_op jit(solution)/shard_map/make_blocks/pallas_call | solution.py:244
Async XLA Ops:
  0.7 34.3 %copy-start = (bf16[8,2,256,256]{3,2,1,0:T(8,128)(2,1)S(1)}, bf16[8,2,256,256]{3,2,1,0:T(8,128)(2,1)}, u32[]{:S(2)}) copy-start(bf16[8,2,256,256]{3,2,1,0:T(8,128)(2,1)} %elem.1) | copy-start | bytes 6291460
  0.7 34.3 %copy-start.1 = (s32[1,16,4]{1,2,0:T(4,128)S(1)}, s32[1,16,4]{1,2,0:T(4,128)}, u32[]{:S(2)}) copy-start(s32[1,16,4]{1,2,0:T(4,128)} %param.8) | copy-start | bytes 772
